TPU v7x, 128 devices: a whole 4x4x4 slice. The times are simulated.
128 devices in a mesh: front: 4 (over z), tile: 32 (over x, y, core).
Axes of the slice: x: 4, y: 4, z: 4, core: 2. Of those that a mesh axis runs over, the one named last changes fastest.
Arguments:
- front_entries: float32 [4, 4096, 4096], P('front', 'tile')
- child_blocks: bfloat16 [512, 64, 256], P(('front', 'tile'))
- child_map: int32 [128, 256], replicated, may hold values from -1 to 4095, as said below
- parent_list: int32 [128, 1], replicated, may hold values from 0 to 3; in each aligned block of 4 rows (0 to 3, 4 to 7, ...) at most 2 rows name the same one
Outputs:
- front_out: float32 [4, 4096, 4096], P('front', 'tile')
Inputs may be any that keep to these rules, and one draw needn't show every extreme that they name: `child_map`: row c gives the parent-front row of each of the 256 rows of child c: live entries come first and are distinct, -1 marks padding, every row has 128 to 256 live entries, and its first entry is 4095. `parent_list`: in each aligned block of 4 rows no front is named more than 2 times.
All inputs are finite; a program needn't handle non-finite values.
Results may differ from a plain program's by a relative error of at most 0.0003.
Values may be sent and summed in bfloat16 or wider, within the bound.
A program may use at most 128 MiB of HBM per device.

v0:
```python
import jax
import jax.numpy as jnp
from jax import lax
from jax.sharding import PartitionSpec as P

FRONT = 4096
PANEL = 512
PANELS = 2
CHILD = 256
BLOCK_ROWS = 64
BLK_DEV = 4
CAPACITY = 2


def routing(child_map, parent_list, front_count, tile_count, group_id):
    child_count = child_map.shape[0]
    fronts = jnp.arange(front_count, dtype=jnp.int32)
    target = parent_list[:, 0]
    blocks = (
        jnp.arange(front_count * tile_count, dtype=jnp.int32)[:, None] * BLK_DEV
        + jnp.arange(BLK_DEV, dtype=jnp.int32)[None, :]
    )
    child_of = blocks % child_count
    part_of = blocks // child_count
    child_ids = jnp.arange(child_count, dtype=jnp.int32)
    dest_front = jnp.sum(jnp.where(child_of[..., None] == child_ids, target, 0), axis=2)
    earlier = jnp.arange(BLK_DEV)[:, None] > jnp.arange(BLK_DEV)[None, :]
    same_dest = dest_front[:, :, None] == dest_front[:, None, :]
    slot_rank = jnp.sum(same_dest & earlier[None], axis=2)
    slot_ids = jnp.arange(CAPACITY, dtype=jnp.int32)
    select = (dest_front[:, None, None, :] == fronts[None, :, None, None]) & (
        slot_rank[:, None, None, :] == slot_ids[None, None, :, None]
    )
    to_group = select[:, group_id]
    slot_live = jnp.any(to_group, axis=2)
    slot_child = jnp.sum(jnp.where(to_group, child_of[:, None, :], 0), axis=2)
    slot_part = jnp.sum(jnp.where(to_group, part_of[:, None, :], 0), axis=2)
    return (select, slot_live, slot_child, slot_part)


def body(front_entries, child_blocks, child_map, parent_list):
    tile_count = lax.axis_size("tile")
    front_count = lax.axis_size("front")
    group_id = lax.axis_index("front")
    tile_id = lax.axis_index("tile")
    rows_dev = front_entries.shape[1]
    first_row = tile_id * rows_dev
    child_count = child_map.shape[0]
    select, slot_live, slot_child, slot_part = routing(
        child_map, parent_list, front_count, tile_count, group_id
    )
    self_dev = group_id * tile_count + tile_id
    own_select = select[self_dev].astype(jnp.bfloat16)
    outgoing = jnp.einsum(
        "dsj,jrk->dsrk", own_select, child_blocks, preferred_element_type=jnp.float32
    ).astype(jnp.bfloat16)
    incoming = lax.all_to_all(outgoing, "front", split_axis=0, concat_axis=0, tiled=True)
    child_hot = (slot_child[..., None] == jnp.arange(child_count, dtype=jnp.int32)).astype(
        jnp.float32
    )
    map_values = jnp.einsum(
        "dsn,nk->dsk", child_hot, child_map.astype(jnp.float32), precision=lax.Precision.HIGHEST
    )
    col_flat = map_values.astype(jnp.int32)
    part_count = CHILD // BLOCK_ROWS
    col_parts = col_flat.reshape(col_flat.shape[0], CAPACITY, part_count, BLOCK_ROWS)
    part_hot = slot_part[..., None] == jnp.arange(part_count, dtype=jnp.int32)
    row_maps = jnp.sum(jnp.where(part_hot[..., None], col_parts, 0), axis=2)
    row_valid = slot_live[..., None] & (row_maps >= 0)
    row_table = jnp.where(row_valid, row_maps, FRONT).reshape(
        front_count, tile_count, CAPACITY, BLOCK_ROWS
    )
    col_table = col_flat.reshape(front_count, tile_count, CAPACITY, CHILD)
    empty_cols = jnp.zeros((FRONT, rows_dev), jnp.float32)
    front_ids = jnp.arange(FRONT, dtype=jnp.int32)
    own_columns = first_row + jnp.arange(rows_dev)
    shards = lax.all_gather(incoming[None], "tile", axis=0, tiled=True)

    def one_tile(tile_step, running):
        child_rows = lax.dynamic_index_in_dim(shards, tile_step, 0, keepdims=False)
        col_maps = lax.dynamic_index_in_dim(col_table, tile_step, 1, keepdims=False)
        matches = (col_maps[..., None] == own_columns[None, None, None, :]).astype(jnp.bfloat16)
        values = jnp.einsum(
            "gsrk,gskc->gsrc", child_rows, matches, preferred_element_type=jnp.float32
        ).astype(jnp.bfloat16)
        targets = lax.dynamic_index_in_dim(row_table, tile_step, 1, keepdims=False)
        row_hot = (targets[..., None] == front_ids).astype(jnp.bfloat16)
        return running + jnp.einsum(
            "gsrf,gsrc->fc", row_hot, values, preferred_element_type=jnp.float32
        )

    extend_cols = lax.fori_loop(0, shards.shape[0], one_tile, empty_cols)
    matrix = front_entries[0] + extend_cols.T
    row_ids = first_row + jnp.arange(rows_dev)
    for panel_no in range(PANELS):
        left_col = panel_no * PANEL
        right_col = left_col + PANEL
        cols_piece = matrix[:, left_col:right_col]
        gathered = lax.all_gather(
            cols_piece.astype(jnp.bfloat16), "tile", axis=0, tiled=True
        ).astype(cols_piece.dtype)
        diag_factor = jnp.linalg.cholesky(gathered[left_col:right_col])
        lower_part = jax.scipy.linalg.solve_triangular(
            diag_factor, gathered[right_col:].T, lower=True
        ).T
        factor = jnp.concatenate([diag_factor, lower_part], 0)
        slice_start = jnp.clip(first_row - left_col, 0, FRONT - left_col - rows_dev)
        own_rows = lax.dynamic_slice_in_dim(factor, slice_start, rows_dev, 0)
        trailing = jnp.where((row_ids >= right_col)[:, None], own_rows, 0.0)
        remainder = matrix[:, right_col:] - jnp.dot(
            trailing, lower_part.T, precision=lax.Precision.HIGHEST
        )
        in_lower = row_ids[:, None] - left_col >= jnp.arange(PANEL)[None, :]
        panel_out = jnp.where(in_lower, own_rows, cols_piece)
        matrix = jnp.concatenate([matrix[:, :left_col], panel_out, remainder], 1)
    return matrix[None]


def solution(mesh):
    return jax.shard_map(
        body,
        mesh=mesh,
        in_specs=(P("front", "tile", None), P(("front", "tile"), None, None), P(), P()),
        out_specs=P("front", "tile", None),
        check_vma=False,
    )
```

profile of v0, /device:TPU:1, one launch (start us, length us, event | category | flops | bytes accessed | tf_op | source)
XLA Modules:
  0.0 746.4 jit_solution(17177670713988524720)
XLA Ops:
  11.6 11.3 %all_to_all.5 = bf16[4,2,64,256]{3,2,1,0:T(8,128)(2,1)} all-to-all(bf16[4,2,64,256]{3,2,1,0:T(8,128)(2,1)S(1)} %copy.98), channel_id=1, replica_groups=mesh['front'=4,'tile'=32] {'front'}, dimensions={0} | all-to-all | bytes 524288 | tf_op jit(solution)/shard_map/all_to_all | solution.py:57
  30.5 46.6 %all-gather.9.cloned.1.call-done = bf16[128,2,64,256]{3,2,1,0:T(8,128)(2,1)} async-done(((bf16[4,2,64,256]{3,2,1,0:T(8,128)(2,1)}), bf16[128,2,64,256]{3,2,1,0:T(8,128)(2,1)}) %all-gather.9.cloned.1.call-update) | async-done | bytes 8388624 | tf_op jit(solution)/shard_map/all_gather | solution.py:77
  77.2 186.3 %while.18 = (s32[]{:T(128)}, f32[4096,128]{1,0:T(8,128)}, s32[4,32,2,64]{3,1,0,2:T(8,128)S(1)}, bf16[32,4,2,64,256]{4,3,2,1,0:T(8,128)(2,1)}, s32[4,32,2,256]{3,...) while((s32[]{:T(128)}, f32[4096,128]{1,0:T(8,128)}, s32[4,32,2,64]{3,1,0,2:T(8,128)S(1)}, ...), condition=%wide.region_7.8_spmd.clone, body=%wide.region_6.7_spmd.clone.sunk | while | flops 573898880 | bytes 4508791 | solution.py:92
  267.6 48.6 %all-gather.5.cloned.1.call-done = bf16[4096,512]{0,1:T(8,128)(2,1)} async-done(((bf16[128,512]{0,1:T(8,128)(2,1)}), bf16[4096,512]{0,1:T(8,128)(2,1)}) %all-gather.5.cloned.1.call-update) | async-done | bytes 4194320 | tf_op jit(solution)/shard_map/all_gather | solution.py:99
  324.8 11.7 %cholesky.286 = f32[128,128]{1,0:T(8,128)S(1)} custom-call(f32[128,128]{1,0:T(8,128)S(1)} %cholesky.426), custom_call_target="Cholesky" | custom-call | tf_op jit(solution)/shard_map/jit(cholesky)/cholesky | solution.py:102
  336.7 9.8 %custom-call.34 = f32[1,128,128]{1,2,0:T(8,128)S(1)} custom-call(f32[1,128,128]{2,1,0:T(8,128)S(1)} %get-tuple-element.280), custom_call_target="InvertDiagBlocksLowerTriangular" | custom-call | tf_op jit(solution)/shard_map/jit(cholesky)/cholesky | solution.py:102
  347.3 12.1 %cholesky.305 = f32[128,128]{1,0:T(8,128)S(1)} custom-call(f32[128,128]{1,0:T(8,128)S(1)} %cholesky.430), custom_call_target="Cholesky" | custom-call | tf_op jit(solution)/shard_map/jit(cholesky)/cholesky | solution.py:102
  359.6 9.8 %custom-call.35 = f32[1,128,128]{1,2,0:T(8,128)S(1)} custom-call(f32[1,128,128]{2,1,0:T(8,128)S(1)} %get-tuple-element.278), custom_call_target="InvertDiagBlocksLowerTriangular" | custom-call | tf_op jit(solution)/shard_map/jit(cholesky)/cholesky | solution.py:102
  374.4 11.7 %cholesky.326 = f32[128,128]{1,0:T(8,128)S(1)} custom-call(f32[128,128]{1,0:T(8,128)S(1)} %cholesky.435), custom_call_target="Cholesky" | custom-call | tf_op jit(solution)/shard_map/jit(cholesky)/cholesky | solution.py:102
  399.1 11.9 %cholesky.343 = f32[128,128]{1,0:T(8,128)S(1)} custom-call(f32[128,128]{1,0:T(8,128)S(1)} %convolution_subtract_fusion.11), custom_call_target="Cholesky" | custom-call | tf_op jit(solution)/shard_map/jit(cholesky)/cholesky | solution.py:102
  419.5 11.4 %while.16 = (s32[]{:T(128)}, f32[512,512]{0,1:T(8,128)}, s32[4,2]{0,1:T(2,128)S(1)}, f32[4,128,128]{2,1,0:T(8,128)S(1)}, s32[]{:T(128)}) while((s32[]{:T(128)}, f32[512,512]{0,1:T(8,128)}, s32[4,2]{0,1:T(2,128)S(1)}, f32[4,128,128]{2,1,0:T(8,128)S(1)}, s32[]{:T(128)}) %tuple.89), condition=%wide.while_cond, body=%wide.while_body.sunk | while | flops 2 | bytes 393329 | solution.py:103
  431.6 40.1 %custom-call.28 = f32[4,128,128]{1,2,0:T(8,128)S(1)} custom-call(f32[4,128,128]{2,1,0:T(8,128)} %copy-done.8), custom_call_target="InvertDiagBlocksLowerTriangular" | custom-call | tf_op jit(solution)/shard_map/jit(_solve_triangular)/triangular_solve | solution.py:103
  493.7 12.4 %convolution_subtract_fusion = f32[128,3584]{0,1:T(8,128)S(1)} fusion(f32[128,3584]{1,0:T(8,128)S(1)} %fusion.90, f32[128,3584]{1,0:T(8,128)S(1)} %fusion.91, f32[128,3584]{1,0:T(8,128)S(1)} %fusion.93, f32[128,3584]{1,0:T(8,128)S(1)} %fusion.50, f32[128,4096]{0,1:T(8,128)S(1)} %copy-done.3, pred[128]{0:T(512)(128)(4,1)S(1)} %broadcast_compare_fusion.1, ...), kind=kOutput, calls=%fused_computation.37 | convolution fusion | flops 2824667136 | bytes 19398788 | tf_op jit(solution)/shard_map/dot_general | solution.py:110
  508.2 48.6 %all-gather.7.cloned.1.call-done = bf16[4096,512]{0,1:T(8,128)(2,1)} async-done(((bf16[128,512]{0,1:T(8,128)(2,1)}), bf16[4096,512]{0,1:T(8,128)(2,1)}) %all-gather.7.cloned.1.call-update) | async-done | bytes 4194320 | tf_op jit(solution)/shard_map/all_gather | solution.py:99
  564.9 11.7 %cholesky.358 = f32[128,128]{1,0:T(8,128)S(1)} custom-call(f32[128,128]{1,0:T(8,128)S(1)} %cholesky.439), custom_call_target="Cholesky" | custom-call | tf_op jit(solution)/shard_map/jit(cholesky)/cholesky | solution.py:102
  576.8 9.8 %custom-call.37 = f32[1,128,128]{1,2,0:T(8,128)S(1)} custom-call(f32[1,128,128]{2,1,0:T(8,128)S(1)} %get-tuple-element.274), custom_call_target="InvertDiagBlocksLowerTriangular" | custom-call | tf_op jit(solution)/shard_map/jit(cholesky)/cholesky | solution.py:102
  587.4 12.1 %cholesky.377 = f32[128,128]{1,0:T(8,128)S(1)} custom-call(f32[128,128]{1,0:T(8,128)S(1)} %cholesky.443), custom_call_target="Cholesky" | custom-call | tf_op jit(solution)/shard_map/jit(cholesky)/cholesky | solution.py:102
  599.6 9.8 %custom-call.38 = f32[1,128,128]{1,2,0:T(8,128)S(1)} custom-call(f32[1,128,128]{2,1,0:T(8,128)S(1)} %get-tuple-element.272), custom_call_target="InvertDiagBlocksLowerTriangular" | custom-call | tf_op jit(solution)/shard_map/jit(cholesky)/cholesky | solution.py:102
  610.5 11.7 %cholesky.398 = f32[128,128]{1,0:T(8,128)S(1)} custom-call(f32[128,128]{1,0:T(8,128)S(1)} %cholesky.448), custom_call_target="Cholesky" | custom-call | tf_op jit(solution)/shard_map/jit(cholesky)/cholesky | solution.py:102
  622.4 9.8 %custom-call.39 = f32[1,128,128]{1,2,0:T(8,128)S(1)} custom-call(f32[1,128,128]{2,1,0:T(8,128)S(1)} %get-tuple-element.270), custom_call_target="InvertDiagBlocksLowerTriangular" | custom-call | tf_op jit(solution)/shard_map/jit(cholesky)/cholesky | solution.py:102
  633.0 11.9 %cholesky.415 = f32[128,128]{1,0:T(8,128)S(1)} custom-call(f32[128,128]{1,0:T(8,128)S(1)} %convolution_subtract_fusion.10), custom_call_target="Cholesky" | custom-call | tf_op jit(solution)/shard_map/jit(cholesky)/cholesky | solution.py:102
  653.5 14.5 %while.17 = (s32[]{:T(128)}, f32[512,512]{0,1:T(8,128)}, s32[4,2]{0,1:T(2,128)S(1)}, f32[4,128,128]{2,1,0:T(8,128)}, s32[]{:T(128)}) while((s32[]{:T(128)}, f32[512,512]{0,1:T(8,128)}, s32[4,2]{0,1:T(2,128)S(1)}, f32[4,128,128]{2,1,0:T(8,128)}, s32[]{:T(128)}) %tuple.102), condition=%wide.while_cond.1, body=%wide.while_body.1.sunk | while | flops 2 | bytes 393329 | solution.py:103
  668.0 40.7 %custom-call.29 = f32[4,128,128]{1,2,0:T(8,128)} custom-call(f32[4,128,128]{2,1,0:T(8,128)} %get-tuple-element.146), custom_call_target="InvertDiagBlocksLowerTriangular" | custom-call | tf_op jit(solution)/shard_map/jit(_solve_triangular)/triangular_solve | solution.py:103
  726.9 10.5 %convolution_subtract_fusion.4 = f32[128,3072]{0,1:T(8,128)S(1)} fusion(f32[128,3072]{1,0:T(8,128)S(1)} %fusion.84, f32[128,3072]{1,0:T(8,128)S(1)} %fusion.85, f32[128,3072]{1,0:T(8,128)S(1)} %fusion.87, f32[128,3072]{1,0:T(8,128)S(1)} %fusion.52, f32[128,3584]{0,1:T(8,128)S(1)} %copy-done.5, pred[128]{0:T(512)(128)(4,1)S(1)} %broadcast_compare_fusion, ...), kind=kOutput, calls=%fused_computation.49 | convolution fusion | flops 2421161984 | bytes 16777348 | tf_op jit(solution)/shard_map/dot_general | solution.py:110
  (389 shorter events, 323.3 us)
Async XLA Ops:
  6.5 21.4 %copy-start.9 = (s32[128,256]{1,0:T(8,128)S(1)}, s32[128,256]{1,0:T(8,128)}, u32[]{:S(2)}) copy-start(s32[128,256]{1,0:T(8,128)} %param.9) | copy-start | bytes 393220
  6.5 70.7 %all-gather.9.cloned.1.call-start = ((), (), s32[]{:S(2)}) async-start(), calls=%async_computation.3 | async-start | bytes 8650752 | tf_op jit(solution)/shard_map/all_gather | solution.py:77
  22.9 293.2 %all-gather.5.cloned.1.call-start = ((), (), s32[]{:S(2)}) async-start(), calls=%async_computation.1 | async-start | bytes 4325376 | tf_op jit(solution)/shard_map/all_gather | solution.py:99
  265.3 1.3 copy-start.2
  267.3 289.5 %all-gather.7.cloned.1.call-start = ((), (), s32[]{:S(2)}) async-start(), calls=%async_computation.2 | async-start | bytes 4325376 | tf_op jit(solution)/shard_map/all_gather | solution.py:99
  416.4 58.7 %slice-start = ((s8[7340032]{0:T(1024)(128)(4,1)}), s8[3145728]{0:T(1024)(128)(4,1)S(1)}, s32[]{:S(2)}) async-start(s8[7340032]{0:T(1024)(128)(4,1)} %bitcast.155), calls=%async_computation.4 | async-start | bytes 6291456
  430.9 0.7 copy-start.8
  471.7 3.4 slice-start.1
  490.8 1.2 copy-start.1
  490.8 2.8 copy-start.3
  491.4 14.7 %copy-start = (f32[3584,512]{0,1:T(8,128)}, f32[3584,512]{0,1:T(8,128)S(1)}, u32[]{:S(2)}) copy-start(f32[3584,512]{0,1:T(8,128)S(1)} %fusion.35) | copy-start | bytes 22020100
  506.0 1.2 copy-start.4
  647.6 1.9 copy-start.6
  650.1 61.7 %slice-start.2 = ((s8[6291456]{0:T(1024)(128)(4,1)}), s8[2097152]{0:T(1024)(128)(4,1)S(1)}, s32[]{:S(2)}) async-start(s8[6291456]{0:T(1024)(128)(4,1)} %bitcast.157), calls=%async_computation.6 | async-start | bytes 4194304
  708.7 2.3 copy-start.7
  708.7 3.2 slice-start.3
  725.4 1.5 copy-start.5
Sparse Core Ops, SparseCore 0:
  23.1 54.0 all-gather.8
  267.4 48.7 all-gather.4
  508.1 48.6 all-gather.6
where the time goes:
time: 756 us; the launch traced here: 746 us
  other arithmetic  265 us (35%)
  matrix products  247 us (33%)
  waiting for transfers between devices  144 us (19%)
  local copies, waits for them, and re-layouts  58.7 us (8%)
  between operations  19.3 us (3%)
  blocking collectives  11.3 us (1%)
    dot_general x32, matrix products, one_tile(): jnp.einsum('gsrf,gsrc->fc', row_hot, values, preferred_element_type=jnp.f...  184 us
    another operation x29, other arithmetic, body(): diag_factor = jnp.linalg.cholesky(gathered[left_col:right_col])  159 us
    all_gather x2, waiting for transfers between devices, body(): lax.all_gather(cols_piece.astype(jnp.bfloat16), 'tile', axis=0, tiled=True)  97.2 us
    another operation x5, other arithmetic, body(): jax.scipy.linalg.solve_triangular(diag_factor, gathered[right_col:].T, lo...  86.6 us
    all_gather x1, waiting for transfers between devices, body(): shards = lax.all_gather(incoming[None], 'tile', axis=0, tiled=True)  46.6 us
    another operation x14, matrix products, body(): jax.scipy.linalg.solve_triangular(diag_factor, gathered[right_col:].T, lo...  30.7 us
    another operation x40, local copies, waits for them, and re-layouts  25.7 us
    dot_general x2, matrix products, body(): jnp.dot(trailing, lower_part.T, precision=lax.Precision.HIGHEST)  22.8 us
  transfers between devices with their start and end apart: 3, of which 3 were waited for; matrix products, arithmetic and copies ran while one was open for 1% of the time, Pallas kernels for 0%

commit v1 on v0

--- a/solution.py
+++ b/solution.py
@@ -71,49 +71,69 @@
         front_count, tile_count, CAPACITY, BLOCK_ROWS
     )
     col_table = col_flat.reshape(front_count, tile_count, CAPACITY, CHILD)
-    empty_cols = jnp.zeros((FRONT, rows_dev), jnp.float32)
-    front_ids = jnp.arange(FRONT, dtype=jnp.int32)
     own_columns = first_row + jnp.arange(rows_dev)
     shards = lax.all_gather(incoming[None], "tile", axis=0, tiled=True)
 
-    def one_tile(tile_step, running):
-        child_rows = lax.dynamic_index_in_dim(shards, tile_step, 0, keepdims=False)
-        col_maps = lax.dynamic_index_in_dim(col_table, tile_step, 1, keepdims=False)
-        matches = (col_maps[..., None] == own_columns[None, None, None, :]).astype(jnp.bfloat16)
-        values = jnp.einsum(
-            "gsrk,gskc->gsrc", child_rows, matches, preferred_element_type=jnp.float32
-        ).astype(jnp.bfloat16)
-        targets = lax.dynamic_index_in_dim(row_table, tile_step, 1, keepdims=False)
-        row_hot = (targets[..., None] == front_ids).astype(jnp.bfloat16)
-        return running + jnp.einsum(
-            "gsrf,gsrc->fc", row_hot, values, preferred_element_type=jnp.float32
-        )
+    def extend_range(f_lo, f_count):
+        front_ids = f_lo + jnp.arange(f_count, dtype=jnp.int32)
 
-    extend_cols = lax.fori_loop(0, shards.shape[0], one_tile, empty_cols)
-    matrix = front_entries[0] + extend_cols.T
+        def one_tile(tile_step, running):
+            child_rows = lax.dynamic_index_in_dim(shards, tile_step, 0, keepdims=False)
+            col_maps = lax.dynamic_index_in_dim(col_table, tile_step, 1, keepdims=False)
+            matches = (col_maps[..., None] == own_columns[None, None, None, :]).astype(
+                jnp.bfloat16
+            )
+            values = jnp.einsum(
+                "gsrk,gskc->gsrc", child_rows, matches, preferred_element_type=jnp.float32
+            ).astype(jnp.bfloat16)
+            targets = lax.dynamic_index_in_dim(row_table, tile_step, 1, keepdims=False)
+            row_hot = (targets[..., None] == front_ids).astype(jnp.bfloat16)
+            return running + jnp.einsum(
+                "gsrf,gsrc->fc", row_hot, values, preferred_element_type=jnp.float32
+            )
+
+        empty = jnp.zeros((f_count, rows_dev), jnp.float32)
+        return lax.fori_loop(0, shards.shape[0], one_tile, empty)
+
+    hi = lax.Precision.HIGHEST
+    split = PANELS * PANEL
+    left_cols = front_entries[0][:, :split] + extend_range(0, split).T
+    gathered = lax.all_gather(left_cols.astype(jnp.bfloat16), "tile", axis=0, tiled=True)
+    right_cols = front_entries[0][:, split:] + extend_range(split, FRONT - split).T
+    matrix = jnp.concatenate([left_cols, right_cols], 1)
     row_ids = first_row + jnp.arange(rows_dev)
+    eye = jnp.eye(PANEL, dtype=jnp.float32)
+    below = gathered[:, :PANEL].astype(jnp.float32)
+    pieces = []
     for panel_no in range(PANELS):
         left_col = panel_no * PANEL
         right_col = left_col + PANEL
-        cols_piece = matrix[:, left_col:right_col]
-        gathered = lax.all_gather(
-            cols_piece.astype(jnp.bfloat16), "tile", axis=0, tiled=True
-        ).astype(cols_piece.dtype)
-        diag_factor = jnp.linalg.cholesky(gathered[left_col:right_col])
-        lower_part = jax.scipy.linalg.solve_triangular(
-            diag_factor, gathered[right_col:].T, lower=True
-        ).T
-        factor = jnp.concatenate([diag_factor, lower_part], 0)
-        slice_start = jnp.clip(first_row - left_col, 0, FRONT - left_col - rows_dev)
-        own_rows = lax.dynamic_slice_in_dim(factor, slice_start, rows_dev, 0)
-        trailing = jnp.where((row_ids >= right_col)[:, None], own_rows, 0.0)
-        remainder = matrix[:, right_col:] - jnp.dot(
-            trailing, lower_part.T, precision=lax.Precision.HIGHEST
-        )
+        diag_factor = jnp.linalg.cholesky(below[:PANEL])
+        inv_factor = jax.scipy.linalg.solve_triangular(diag_factor, eye, lower=True)
+        lower_rows = below[PANEL:]
+        cols_piece = matrix[:, :PANEL]
+        own_lower = jnp.dot(cols_piece, inv_factor.T, precision=hi)
+        slice_start = jnp.clip(first_row - left_col, 0, PANEL - rows_dev)
+        diag_rows = lax.dynamic_slice_in_dim(diag_factor, slice_start, rows_dev, 0)
+        own_rows = jnp.where((row_ids < right_col)[:, None], diag_rows, own_lower)
+        trailing = jnp.where((row_ids >= right_col)[:, None], own_lower, 0.0)
+        weights = jnp.dot(trailing, inv_factor, precision=hi)
+        remainder = matrix[:, PANEL:] - jnp.dot(weights, lower_rows.T, precision=hi)
         in_lower = row_ids[:, None] - left_col >= jnp.arange(PANEL)[None, :]
-        panel_out = jnp.where(in_lower, own_rows, cols_piece)
-        matrix = jnp.concatenate([matrix[:, :left_col], panel_out, remainder], 1)
-    return matrix[None]
+        pieces.append(jnp.where(in_lower, own_rows, cols_piece))
+        matrix = remainder
+        if panel_no + 1 < PANELS:
+            next_left = right_col
+            next_cols = gathered[next_left:, next_left:next_left + PANEL].astype(jnp.float32)
+            top_lower = lower_rows[:PANEL]
+            coupling = jnp.dot(
+                inv_factor.T,
+                jnp.dot(inv_factor, top_lower.T, precision=hi),
+                precision=hi,
+            )
+            below = next_cols - jnp.dot(lower_rows, coupling, precision=hi)
+    pieces.append(matrix)
+    return jnp.concatenate(pieces, 1)[None]
 
 
 def solution(mesh):

time: 756 us -> 746 us (0.987)
  waiting for transfers between devices: 144 us -> 43.9 us
  matrix products: 247 us -> 316 us
  other arithmetic: 265 us -> 287 us
    all_gather x2 -> x1, waiting for transfers between devices: 97.2 us -> 0.01 us  [body(): lax.all_gather(left_cols.astype(jnp.bfloat16), 'tile', axis=0, tiled=True)]
    dot_general x32 -> x64, matrix products: 184 us -> 253 us  [one_tile(): jnp.einsum('gsrf,gsrc->fc', row_hot, values, preferred_element_type=jnp.f...]
    eq x0 -> x128, local copies, waits for them, and re-layouts: none -> 19.3 us  [the longest x64 19.1 us: one_tile(): col_maps[..., None] == own_columns[None, None, None, :]]
    dot_general x2 -> x9, matrix products: 22.8 us -> 40.9 us  [the longest x2 18.6 us: body(): remainder = matrix[:, PANEL:] - jnp.dot(weights, lower_rows.T, precision=hi)]
    another operation x26, matrix products: 38.7 us -> 20.6 us  [the longest x12 10.6 us: body(): diag_factor = jnp.linalg.cholesky(below[:PANEL])]
    add x33 -> x65, other arithmetic: 0.11 us -> 17.7 us  [body(): row_ids = first_row + jnp.arange(rows_dev)]
    transpose x4 -> x0, local copies, waits for them, and re-layouts: 11.4 us -> none  [body(): gathered[right_col:]]
    another operation x67 -> x65, local copies, waits for them, and re-layouts: 30.6 us -> 25.6 us  [the longest x43 20.8 us: body(): inv_factor = jax.scipy.linalg.solve_triangular(diag_factor, eye, lower=True)]
  transfers between devices with their start and end apart: 3 -> 2, of which waited for: 3 -> 1; matrix products, arithmetic and copies ran while one was open for 1% -> 28% of each run, Pallas kernels for 0% -> 0%
where the time goes in v1:
time: 746 us; the launch traced here: 735 us
  matrix products  316 us (42%)
  other arithmetic  287 us (38%)
  local copies, waits for them, and re-layouts  56.8 us (8%)
  waiting for transfers between devices  43.9 us (6%)
  between operations  19.7 us (3%)
  blocking collectives  11.3 us (2%)
    dot_general x64, matrix products, one_tile(): jnp.einsum('gsrf,gsrc->fc', row_hot, values, preferred_element_type=jnp.f...  253 us
    another operation x29, other arithmetic, body(): diag_factor = jnp.linalg.cholesky(below[:PANEL])  165 us
    another operation x5, other arithmetic, body(): inv_factor = jax.scipy.linalg.solve_triangular(diag_factor, eye, lower=True)  82.1 us
    all_gather x1, waiting for transfers between devices, body(): shards = lax.all_gather(incoming[None], 'tile', axis=0, tiled=True)  43.9 us
    another operation x43, local copies, waits for them, and re-layouts, body(): inv_factor = jax.scipy.linalg.solve_triangular(diag_factor, eye, lower=True)  20.8 us
    eq x64, local copies, waits for them, and re-layouts, one_tile(): col_maps[..., None] == own_columns[None, None, None, :]  19.1 us
    dot_general x2, matrix products, body(): remainder = matrix[:, PANEL:] - jnp.dot(weights, lower_rows.T, precision=hi)  18.6 us
    add x65, other arithmetic, body(): row_ids = first_row + jnp.arange(rows_dev)  17.7 us
  transfers between devices with their start and end apart: 2, of which 1 were waited for; matrix products, arithmetic and copies ran while one was open for 28% of the time, Pallas kernels for 0%

profile of v1, /device:TPU:1, one launch (start us, length us, event | category | flops | bytes accessed | tf_op | source)
XLA Modules:
  0.0 735.2 jit_solution(7317852413350347162)
XLA Ops:
  11.6 11.3 %all_to_all.5 = bf16[4,2,64,256]{3,2,1,0:T(8,128)(2,1)} all-to-all(bf16[4,2,64,256]{3,2,1,0:T(8,128)(2,1)S(1)} %copy.96), channel_id=1, replica_groups=mesh['front'=4,'tile'=32] {'front'}, dimensions={0} | all-to-all | bytes 524288 | tf_op jit(solution)/shard_map/all_to_all | solution.py:57
  33.3 43.9 %all-gather.6.cloned.1.call-done = bf16[128,2,64,256]{3,2,1,0:T(8,128)(2,1)} async-done(((bf16[4,2,64,256]{3,2,1,0:T(8,128)(2,1)}), bf16[128,2,64,256]{3,2,1,0:T(8,128)(2,1)}) %all-gather.6.cloned.1.call-update) | async-done | bytes 8388624 | tf_op jit(solution)/shard_map/all_gather | solution.py:75
  77.2 97.5 %while.32 = (s32[]{:T(128)}, f32[1024,128]{1,0:T(8,128)}, s32[4,32,2,64]{3,2,0,1:T(2,128)S(1)}, bf16[32,4,2,64,256]{4,3,2,1,0:T(8,128)(2,1)}, s32[4,32,2,256]{3,...) while((s32[]{:T(128)}, f32[1024,128]{1,0:T(8,128)}, s32[4,32,2,64]{3,2,0,1:T(2,128)S(1)}, ...), condition=%wide.region_7.8_spmd.clone, body=%wide.region_6.7_spmd.clone.sunk | while | flops 168886400 | bytes 1342583 | solution.py:96
  176.7 192.5 %while.33 = (s32[]{:T(128)}, f32[3072,128]{1,0:T(8,128)}, s32[4,32,2,64]{3,2,0,1:T(2,128)S(1)}, bf16[32,4,2,64,256]{4,3,2,1,0:T(8,128)(2,1)}, s32[4,32,2,256]{3,...) while((s32[]{:T(128)}, f32[3072,128]{1,0:T(8,128)}, s32[4,32,2,64]{3,2,0,1:T(2,128)S(1)}, ...), condition=%wide.region_17.20_spmd.clone, body=%wide.region_16.19_spmd.clone.sunk | while | flops 438897792 | bytes 3464311 | solution.py:96
  374.7 11.7 %cholesky.286 = f32[128,128]{1,0:T(8,128)S(1)} custom-call(f32[128,128]{1,0:T(8,128)S(1)} %cholesky.426), custom_call_target="Cholesky" | custom-call | tf_op jit(solution)/shard_map/jit(cholesky)/cholesky | solution.py:111
  386.5 9.8 %custom-call.29 = f32[1,128,128]{1,2,0:T(8,128)S(1)} custom-call(f32[1,128,128]{2,1,0:T(8,128)S(1)} %get-tuple-element.470), custom_call_target="InvertDiagBlocksLowerTriangular" | custom-call | tf_op jit(solution)/shard_map/jit(cholesky)/cholesky | solution.py:111
  397.4 11.7 %cholesky.305 = f32[128,128]{1,0:T(8,128)S(1)} custom-call(f32[128,128]{1,0:T(8,128)S(1)} %cholesky.430), custom_call_target="Cholesky" | custom-call | tf_op jit(solution)/shard_map/jit(cholesky)/cholesky | solution.py:111
  409.2 10.0 %custom-call.30 = f32[1,128,128]{1,2,0:T(8,128)S(1)} custom-call(f32[1,128,128]{2,1,0:T(8,128)S(1)} %get-tuple-element.468), custom_call_target="InvertDiagBlocksLowerTriangular" | custom-call | tf_op jit(solution)/shard_map/jit(cholesky)/cholesky | solution.py:111
  420.2 11.7 %cholesky.326 = f32[128,128]{1,0:T(8,128)S(1)} custom-call(f32[128,128]{1,0:T(8,128)S(1)} %cholesky.435), custom_call_target="Cholesky" | custom-call | tf_op jit(solution)/shard_map/jit(cholesky)/cholesky | solution.py:111
  432.1 9.8 %custom-call.31 = f32[1,128,128]{1,2,0:T(8,128)S(1)} custom-call(f32[1,128,128]{2,1,0:T(8,128)S(1)} %get-tuple-element.466), custom_call_target="InvertDiagBlocksLowerTriangular" | custom-call | tf_op jit(solution)/shard_map/jit(cholesky)/cholesky | solution.py:111
  442.7 12.1 %cholesky.343 = f32[128,128]{1,0:T(8,128)S(1)} custom-call(f32[128,128]{1,0:T(8,128)S(1)} %convolution_subtract_fusion.12), custom_call_target="Cholesky" | custom-call | tf_op jit(solution)/shard_map/jit(cholesky)/cholesky | solution.py:111
  460.8 8.6 %while.34 = (s32[]{:T(128)}, f32[512,512]{0,1:T(8,128)S(1)}, s32[4,2]{0,1:T(2,128)S(1)}, f32[4,128,128]{2,1,0:T(8,128)S(1)}, s32[]{:T(128)}) while((s32[]{:T(128)}, f32[512,512]{0,1:T(8,128)S(1)}, s32[4,2]{0,1:T(2,128)S(1)}, f32[4,128,128]{2,1,0:T(8,128)S(1)}, s32[]{:T(128)}) %tuple.127), condition=%wide.while_cond, body=%wide.while_body.sunk | while | flops 2 | bytes 393329 | solution.py:112
  469.4 39.3 %custom-call.32 = f32[4,128,128]{1,2,0:T(8,128)S(1)} custom-call(f32[4,128,128]{2,1,0:T(8,128)S(1)} %get-tuple-element.323), custom_call_target="InvertDiagBlocksLowerTriangular" | custom-call | tf_op jit(solution)/shard_map/jit(_solve_triangular)/triangular_solve | solution.py:112
  516.9 9.3 %convert_subtract_fusion = f32[3584,512]{0,1:T(8,128)S(1)} fusion(f32[512,512]{1,0:T(8,128)S(1)} %fusion.145, bf16[4096,1024]{0,1:T(8,128)(2,1)} %all-gather.4.cloned.1.call-done), kind=kOutput, calls=%fused_computation.40 | convolution fusion | flops 11277959168 | bytes 15728640 | tf_op jit(solution)/shard_map/dot_general | solution.py:134
  532.9 11.7 %cholesky.358 = f32[128,128]{1,0:T(8,128)S(1)} custom-call(f32[128,128]{1,0:T(8,128)S(1)} %cholesky.439), custom_call_target="Cholesky" | custom-call | tf_op jit(solution)/shard_map/jit(cholesky)/cholesky | solution.py:111
  544.8 9.8 %custom-call.33 = f32[1,128,128]{1,2,0:T(8,128)S(1)} custom-call(f32[1,128,128]{2,1,0:T(8,128)S(1)} %get-tuple-element.464), custom_call_target="InvertDiagBlocksLowerTriangular" | custom-call | tf_op jit(solution)/shard_map/jit(cholesky)/cholesky | solution.py:111
  558.3 11.7 %cholesky.377 = f32[128,128]{1,0:T(8,128)S(1)} custom-call(f32[128,128]{1,0:T(8,128)S(1)} %cholesky.443), custom_call_target="Cholesky" | custom-call | tf_op jit(solution)/shard_map/jit(cholesky)/cholesky | solution.py:111
  570.7 11.0 %custom-call.34 = f32[1,128,128]{1,2,0:T(8,128)S(1)} custom-call(f32[1,128,128]{2,1,0:T(8,128)} %get-tuple-element.462), custom_call_target="InvertDiagBlocksLowerTriangular" | custom-call | tf_op jit(solution)/shard_map/jit(cholesky)/cholesky | solution.py:111
  585.1 13.2 %cholesky.398 = f32[128,128]{1,0:T(8,128)} custom-call(f32[128,128]{1,0:T(8,128)} %cholesky.448), custom_call_target="Cholesky" | custom-call | tf_op jit(solution)/shard_map/jit(cholesky)/cholesky | solution.py:111
  602.1 11.3 %custom-call.35 = f32[1,128,128]{1,2,0:T(8,128)} custom-call(f32[1,128,128]{2,1,0:T(8,128)} %get-tuple-element.460), custom_call_target="InvertDiagBlocksLowerTriangular" | custom-call | tf_op jit(solution)/shard_map/jit(cholesky)/cholesky | solution.py:111
  615.9 11.9 %cholesky.415 = f32[128,128]{1,0:T(8,128)S(1)} custom-call(f32[128,128]{1,0:T(8,128)S(1)} %convolution_subtract_fusion.11), custom_call_target="Cholesky" | custom-call | tf_op jit(solution)/shard_map/jit(cholesky)/cholesky | solution.py:111
  642.4 12.4 %while.35 = (s32[]{:T(128)}, f32[512,512]{0,1:T(8,128)}, s32[4,2]{0,1:T(2,128)S(1)}, f32[4,128,128]{2,1,0:T(8,128)S(1)}, s32[]{:T(128)}) while((s32[]{:T(128)}, f32[512,512]{0,1:T(8,128)}, s32[4,2]{0,1:T(2,128)S(1)}, f32[4,128,128]{2,1,0:T(8,128)S(1)}, s32[]{:T(128)}) %tuple.142), condition=%wide.while_cond.clone, body=%wide.while_body.clone.sunk | while | flops 2 | bytes 393329 | solution.py:112
  654.8 39.3 %custom-call.36 = f32[4,128,128]{1,2,0:T(8,128)S(1)} custom-call(f32[4,128,128]{2,1,0:T(8,128)S(1)} %get-tuple-element.324), custom_call_target="InvertDiagBlocksLowerTriangular" | custom-call | tf_op jit(solution)/shard_map/jit(_solve_triangular)/triangular_solve | solution.py:112
  711.3 12.4 %fusion.48 = f32[128,3072]{0,1:T(8,128)S(1)} fusion(f32[128,512]{1,0:T(8,128)S(1)} %fusion.68, f32[3584,512]{0,1:T(8,128)} %copy-done, f32[128,3584]{0,1:T(8,128)S(1)} %convolution_subtract_fusion), kind=kOutput, calls=%fused_computation.44 | convolution fusion | flops 2416312320 | bytes 9699328 | tf_op jit(solution)/shard_map/dot_general | solution.py:121
  (495 shorter events, 401.9 us)
Async XLA Ops:
  6.5 21.4 %copy-start.13 = (s32[128,256]{1,0:T(8,128)S(1)}, s32[128,256]{1,0:T(8,128)}, u32[]{:S(2)}) copy-start(s32[128,256]{1,0:T(8,128)} %param.13) | copy-start | bytes 393220
  6.5 70.7 %all-gather.6.cloned.1.call-start = ((), (), s32[]{:S(2)}) async-start(), calls=%async_computation.2 | async-start | bytes 8650752 | tf_op jit(solution)/shard_map/all_gather | solution.py:75
  22.9 349.0 %all-gather.4.cloned.1.call-start = ((), (), s32[]{:S(2)}) async-start(), calls=%async_computation.1 | async-start | bytes 8650752 | tf_op jit(solution)/shard_map/all_gather | solution.py:101
  432.0 28.8 %copy-start.20 = (s32[4]{0:T(128)S(1)}, s32[4]{0:T(128)}, u32[]{:S(2)}) copy-start(s32[4]{0:T(128)} %iota_multiply_fusion) | copy-start | bytes 52
  508.7 1.8 copy-start.11
  510.0 5.0 copy-start.2
  510.9 4.1 copy-start.5
  512.9 4.0 copy-start.8
  526.2 3.0 copy-start
  554.7 73.7 %copy-start.3 = (f32[128,512]{1,0:T(8,128)S(1)}, f32[128,512]{1,0:T(8,128)}, u32[]{:S(2)}) copy-start(f32[128,512]{1,0:T(8,128)} %copy-done.2) | copy-start | bytes 786436
  554.7 73.7 %copy-start.4 = (f32[128,1024]{0,1:T(8,128)S(1)}, f32[128,1024]{0,1:T(8,128)}, u32[]{:S(2)}) copy-start(f32[128,1024]{0,1:T(8,128)} %get-tuple-element.452) | copy-start | bytes 1572868
  554.7 73.7 %copy-start.6 = (f32[128,512]{1,0:T(8,128)S(1)}, f32[128,512]{1,0:T(8,128)}, u32[]{:S(2)}) copy-start(f32[128,512]{1,0:T(8,128)} %copy-done.5) | copy-start | bytes 786436
  557.6 0.7 copy-start.9
  628.4 9.2 %copy-start.18 = (f32[128]{0:T(128)S(1)}, f32[128]{0:T(128)}, u32[]{:S(2)}) copy-start(f32[128]{0:T(128)} %select_reduce_fusion.2) | copy-start | bytes 1540
  695.9 4.4 copy-start.1
  695.9 4.4 copy-start.10
  700.2 6.1 copy-start.12
  706.4 3.1 copy-start.19
  711.2 12.5 %copy-start.7 = (f32[128,512]{0,1:T(8,128)S(1)}, f32[128,512]{0,1:T(8,128)}, u32[]{:S(2)}) copy-start(f32[128,512]{0,1:T(8,128)} %copy.105) | copy-start | bytes 786436
  711.3 12.5 %copy-start.16 = (pred[128]{0:T(512)(128)(4,1)S(1)}, pred[128]{0:T(512)(128)(4,1)}, u32[]{:S(2)}) copy-start(pred[128]{0:T(512)(128)(4,1)} %get-tuple-element.482) | copy-start | bytes 388
  711.3 12.5 %copy-start.17 = (s32[128]{0:T(128)S(1)}, s32[128]{0:T(128)}, u32[]{:S(2)}) copy-start(s32[128]{0:T(128)} %get-tuple-element.477) | copy-start | bytes 1540
  711.3 13.7 %copy-start.14 = (pred[128]{0:T(512)(128)(4,1)S(1)}, pred[128]{0:T(512)(128)(4,1)}, u32[]{:S(2)}) copy-start(pred[128]{0:T(512)(128)(4,1)} %get-tuple-element.480) | copy-start | bytes 388
  711.3 13.7 %copy-start.15 = (s32[128]{0:T(128)S(1)}, s32[128]{0:T(128)}, u32[]{:S(2)}) copy-start(s32[128]{0:T(128)} %get-tuple-element.478) | copy-start | bytes 1540
Sparse Core Ops, SparseCore 0:
  23.1 54.0 all-gather.5
  176.9 59.0 all-gather.3
